TPU v7x, 256 devices: a whole 4x4x8 slice. The times are simulated.
256 devices in a mesh: prow: 16 (over x, y), pcol: 16 (over z, core).
Axes of the slice: x: 4, y: 4, z: 8, core: 2. Of those that a mesh axis runs over, the one named last changes fastest.
Arguments:
- left_factor: bfloat16 [64, 32, 2048, 128], P('prow', 'pcol'), may hold values from -0.8984375 to 0.8984375
- right_factor: bfloat16 [64, 32, 2048, 128], P('prow', 'pcol'), may hold values from -0.8984375 to 0.8984375
- pivot_left: bfloat16 [32, 2048, 128], P('pcol', 'prow'), may hold values from -0.8984375 to 0.8984375
- pivot_right: bfloat16 [32, 2048, 128], P('pcol', 'prow'), may hold values from -0.8984375 to 0.8984375
- target_left: bfloat16 [2048, 64, 128], P('pcol', 'prow'), may hold values from -6 to 6
- target_right: bfloat16 [2048, 64, 128], P('pcol', 'prow'), may hold values from -6 to 6
- probe: bfloat16 [2048, 128], P('prow'), may hold values from -6 to 6
- ranks: int32 [64, 32], P('prow', 'pcol'), may hold values from 16 to 128
Outputs:
- basis: float32 [2048, 64, 128], P('pcol', 'prow')
- coefficient: float32 [2048, 64, 128], P('pcol', 'prow')
All inputs are finite; a program needn't handle non-finite values.
Results may differ from a plain program's by a relative error of at most 0.0038.
Values may be sent and summed in bfloat16 or wider, within the bound.
No kernel may reach another device: no remote copies, remote signals or barrier semaphores. Data moves between devices by JAX's collectives and lax.ppermute only.
A program may use at most 64 MiB of HBM per device.

v0:
```python
import jax
import jax.numpy as jnp
from jax import lax
from jax.sharding import PartitionSpec as P

exact_mode = lax.Precision.HIGHEST


def solve_rows(lower_factor, samples):
    stacked = jnp.transpose(samples, (1, 0, 2))
    solved = lax.linalg.triangular_solve(
        lower_factor, stacked, left_side=False, lower=True, transpose_a=True
    )
    return jnp.transpose(solved, (1, 0, 2))


def per_device(
    left_factor, right_factor, pivot_left, pivot_right, target_left, target_right, probe, ranks
):
    pivot_whole, pivot_other, probe_whole = (
        lax.all_gather(pivot_left, "prow", axis=1, tiled=True),
        lax.all_gather(pivot_right, "prow", axis=1, tiled=True),
        lax.all_gather(probe, "prow", axis=0, tiled=True),
    )
    order_full = left_factor.shape[2]
    rank_span = left_factor.shape[3]
    row_count = target_left.shape[0]
    first_row = lax.axis_index("pcol") * row_count
    probe_slice = lax.dynamic_slice_in_dim(probe_whole, first_row, row_count, 0)
    sample_part = jnp.einsum(
        "bir,bs->irs", target_right, probe_slice, preferred_element_type=jnp.float32
    )
    target_sample = lax.psum(sample_part, "pcol")
    pivot_sample = jnp.einsum(
        "jbr,bs->jrs", pivot_whole, probe_whole, preferred_element_type=jnp.float32
    )
    rank_index = lax.broadcasted_iota(jnp.int32, ranks.shape + (rank_span,), 2)
    rank_mask = (rank_index < ranks[:, :, None]).astype(jnp.float32)
    coupling = jnp.einsum(
        "ijbr,jbs->ijrs", right_factor, pivot_other, preferred_element_type=jnp.float32
    )
    coupling = coupling * rank_mask[:, :, :, None]
    weights = jnp.einsum("ijrs,jst->ijrt", coupling, pivot_sample, precision=exact_mode).astype(
        jnp.bfloat16
    )
    target_term = jnp.einsum(
        "bis,ist->bit", target_left.astype(jnp.float32), target_sample, precision=exact_mode
    )
    samples_own = (
        lax.psum_scatter(
            -jnp.einsum("ijbr,ijrt->bit", left_factor, weights, preferred_element_type=jnp.float32),
            "pcol",
            scatter_dimension=0,
            tiled=True,
        )
        + target_term
    )
    gram_part = jnp.einsum("bir,bis->irs", samples_own, samples_own, precision=exact_mode)
    gram_matrix = lax.psum(gram_part, "pcol") / order_full
    lower_factor = jnp.linalg.cholesky(gram_matrix)
    basis_rows = solve_rows(lower_factor, samples_own)
    basis_full = lax.all_gather(basis_rows.astype(jnp.bfloat16), "pcol", axis=0, tiled=True)
    basis_half = basis_rows.astype(jnp.bfloat16)
    correlation = jnp.einsum(
        "ijbr,bit->ijrt", left_factor, basis_full, preferred_element_type=jnp.float32
    )
    reduced = jnp.einsum("ijrs,ijrt->ijst", coupling, correlation, precision=exact_mode).astype(
        jnp.bfloat16
    )
    correlation_part = jnp.einsum(
        "bis,bit->ist", target_left, basis_half, preferred_element_type=jnp.float32
    )
    target_correlation = lax.psum(correlation_part, "pcol").astype(jnp.bfloat16)
    projected = lax.psum_scatter(
        -jnp.einsum("jbs,ijst->bit", pivot_whole, reduced, preferred_element_type=jnp.float32),
        "pcol",
        scatter_dimension=0,
        tiled=True,
    )
    own_term = jnp.einsum(
        "bis,ist->bit", target_right, target_correlation, preferred_element_type=jnp.float32
    )
    coefficient = (projected + own_term) / order_full
    return (basis_rows, coefficient)


def solution(mesh):
    in_specs = (
        P("prow", "pcol", None, None),
        P("prow", "pcol", None, None),
        P("pcol", "prow", None),
        P("pcol", "prow", None),
        P("pcol", "prow", None),
        P("pcol", "prow", None),
        P("prow", None),
        P("prow", "pcol"),
    )
    out_specs = (P("pcol", "prow", None), P("pcol", "prow", None))
    return jax.shard_map(
        per_device, mesh=mesh, in_specs=in_specs, out_specs=out_specs, check_vma=False
    )
```

profile of v0, /device:TPU:6, one launch (start us, length us, event | category | flops | bytes accessed | tf_op | source)
XLA Modules:
  0.0 534.8 jit_solution(9930926881617621154)
XLA Ops:
  8.1 0.7 all-gather.4.cloned.1.call-update
  8.8 1.6 copy.21
  10.4 24.0 %all_gather.13 = bf16[2048,128]{1,0:T(8,128)(2,1)S(1)} all-gather(bf16[128,128]{1,0:T(8,128)(2,1)} %param.14), channel_id=1, replica_groups=mesh['prow'=16,'pcol'=16] {'prow'}, dimensions={0}, use_global_device_ids=true | all-gather | bytes 557056 | tf_op jit(solution)/shard_map/all_gather | solution.py:23
  34.4 1.8 convolution_bitcast_fusion.4
  36.3 0.8 fusion.32
  37.1 24.4 %all-gather.4.cloned.1.call-done = bf16[2,2048,128]{2,1,0:T(8,128)(2,1)} async-done(((bf16[2,128,128]{2,1,0:T(8,128)(2,1)}), bf16[2,2048,128]{2,1,0:T(8,128)(2,1)}) %all-gather.4.cloned.1.call-update) | async-done | bytes 1048592 | tf_op jit(solution)/shard_map/all_gather | solution.py:21
  61.4 1.7 convolution_bitcast_fusion.5
  63.1 48.8 %all-gather.6.cloned.1.call-done = bf16[2,2048,128]{1,2,0:T(8,128)(2,1)} async-done(((bf16[2,128,128]{1,2,0:T(8,128)(2,1)}), bf16[2,2048,128]{1,2,0:T(8,128)(2,1)}) %all-gather.6.cloned.1.call-update) | async-done | bytes 1048592 | tf_op jit(solution)/shard_map/all_gather | solution.py:22
  112.0 3.4 fusion.9
  115.4 0.6 fusion.12
  116.0 3.4 fusion.1
  119.5 27.8 %all-reduce.4.cloned.1.call-done = f32[4,128,128]{1,2,0:T(8,128)} async-done(((f32[4,128,128]{1,2,0:T(8,128)}), f32[4,128,128]{1,2,0:T(8,128)}) %all-reduce.4.cloned.1.call-update) | async-done | bytes 262160 | tf_op jit(solution)/shard_map/psum | solution.py:33
  147.4 66.3 %reduce-scatter.3.cloned.1.call-done = f32[128,4,128]{0,2,1:T(8,128)} async-done(((f32[2048,4,128]{0,2,1:T(8,128)}), f32[128,4,128]{0,2,1:T(8,128)}) %reduce-scatter.3.cloned.1.call-update) | async-done | bytes 262160 | tf_op jit(solution)/shard_map/reduce_scatter | solution.py:50
  213.6 1.4 fusion.13
  215.1 1.4 fusion.35
  216.6 107.9 %all-reduce.6.cloned.1.call-done = f32[4,128,128]{1,2,0:T(8,128)} async-done(((f32[4,128,128]{1,2,0:T(8,128)}), f32[4,128,128]{1,2,0:T(8,128)}) %all-reduce.6.cloned.1.call-update) | async-done | bytes 262160 | tf_op jit(solution)/shard_map/psum | solution.py:59
  324.5 1.0 broadcast_multiply_fusion
  325.6 1.0 fusion.23
  326.6 46.9 %custom-call.7 = f32[4,128,128]{2,1,0:T(8,128)S(1)} custom-call(f32[4,128,128]{2,1,0:T(8,128)S(1)} %fusion.23), custom_call_target="Cholesky" | custom-call | tf_op jit(solution)/shard_map/jit(cholesky)/cholesky | solution.py:60
  373.8 39.3 %custom-call.8 = f32[4,1,128,128]{2,3,1,0:T(8,128)S(1)} custom-call(f32[4,1,128,128]{3,2,1,0:T(8,128)S(1)} %select_bitcast_fusion), custom_call_target="InvertDiagBlocksLowerTriangular" | custom-call | tf_op jit(solution)/shard_map/triangular_solve | solution.py:11
  413.1 1.3 fusion.34
  414.6 40.2 %all-gather.8.cloned.1.call-done = bf16[2048,4,128]{2,0,1:T(8,128)(2,1)} async-done(((bf16[128,4,128]{2,0,1:T(8,128)(2,1)}), bf16[2048,4,128]{2,0,1:T(8,128)(2,1)}) %all-gather.8.cloned.1.call-update) | async-done | bytes 2097168 | tf_op jit(solution)/shard_map/all_gather | solution.py:62
  454.8 3.8 fusion.4
  458.5 0.4 copy.64
  458.9 1.2 convolution_convert_fusion.1
  460.2 2.7 fusion
  462.9 0.2 convolution_bitcast_fusion.3
  463.1 0.9 copy.30
  464.0 49.8 %all-reduce.7 = bf16[4,128,128]{1,2,0:T(8,128)(2,1)S(1)} all-reduce(f32[4,128,128]{1,2,0:T(8,128)S(1)} %convolution_bitcast_fusion.3), channel_id=1, replica_groups=mesh['prow'=16,'pcol'=16] {'pcol'}, use_global_device_ids=true, to_apply=%region_6.7 | all-reduce | flops 65536 | bytes 393216 | tf_op jit(solution)/shard_map/psum | solution.py:73
  513.8 11.4 %reduce-scatter.5.cloned.1.call-done = f32[128,4,128]{0,2,1:T(8,128)} async-done(((f32[2048,4,128]{0,2,1:T(8,128)}), f32[128,4,128]{0,2,1:T(8,128)}) %reduce-scatter.5.cloned.1.call-update) | async-done | bytes 262160 | tf_op jit(solution)/shard_map/reduce_scatter | solution.py:74
  525.2 1.2 fusion.15
  526.3 0.8 copy.31
  (29 shorter events, 1.0 us)
Async XLA Ops:
  8.0 205.7 %copy-start = (bf16[128,4,128]{2,1,0:T(4,128)(2,1)S(1)}, bf16[128,4,128]{2,1,0:T(4,128)(2,1)}, u32[]{:S(2)}) copy-start(bf16[128,4,128]{2,1,0:T(4,128)(2,1)} %param.12) | copy-start | bytes 393220
  8.0 53.4 %all-gather.4.cloned.1.call-start = ((), (), s32[]{:S(2)}) async-start(), calls=%async_computation.2 | async-start | bytes 1114112 | tf_op jit(solution)/shard_map/all_gather | solution.py:21
  8.7 103.2 %all-gather.6.cloned.1.call-start = ((), (), s32[]{:S(2)}) async-start(), calls=%async_computation.3 | async-start | bytes 1114112 | tf_op jit(solution)/shard_map/all_gather | solution.py:22
  10.4 137.0 %all-reduce.4.cloned.1.call-start = ((), (), s32[]{:S(2)}) async-start(), calls=%async_computation.5 | async-start | bytes 524288 | tf_op jit(solution)/shard_map/psum | solution.py:33
  36.2 177.4 %reduce-scatter.3.cloned.1.call-start = ((), (), s32[]{:S(2)}) async-start(), calls=%async_computation.4 | async-start | bytes 4456448 | tf_op jit(solution)/shard_map/reduce_scatter | solution.py:50
  112.0 4.0 copy-start.1
  119.5 205.0 %all-reduce.6.cloned.1.call-start = ((), (), s32[]{:S(2)}) async-start(), calls=%async_computation.6 | async-start | bytes 524288 | tf_op jit(solution)/shard_map/psum | solution.py:59
  216.5 238.3 %all-gather.8.cloned.1.call-start = ((), (), s32[]{:S(2)}) async-start(), calls=%async_computation.7 | async-start | bytes 2228224 | tf_op jit(solution)/shard_map/all_gather | solution.py:62
  414.4 45.8 %copy-start.2 = (bf16[2,2048,128]{2,1,0:T(8,128)(2,1)S(1)}, bf16[2,2048,128]{2,1,0:T(8,128)(2,1)}, u32[]{:S(2)}) copy-start(bf16[2,2048,128]{2,1,0:T(8,128)(2,1)} %all-gather.4.cloned.1.call-done) | copy-start | bytes 3145732
  414.4 110.8 %reduce-scatter.5.cloned.1.call-start = ((), (), s32[]{:S(2)}) async-start(), calls=%async_computation.8 | async-start | bytes 4456448 | tf_op jit(solution)/shard_map/reduce_scatter | solution.py:74
  460.2 2.7 copy-start.3
  462.9 62.3 %copy-start.4 = (bf16[128,4,128]{2,1,0:T(4,128)(2,1)S(1)}, bf16[128,4,128]{2,1,0:T(4,128)(2,1)}, u32[]{:S(2)}) copy-start(bf16[128,4,128]{2,1,0:T(4,128)(2,1)} %param.13) | copy-start | bytes 393220
Sparse Core Ops, SparseCore 0:
  11.3 50.0 all-gather.3
  64.4 47.5 all-gather.5
Sparse Core Ops, SparseCore 1:
  36.3 111.0 all-reduce.3
  149.8 63.8 reduce-scatter.2
  216.5 107.9 all-reduce.5
  414.4 40.3 all-gather.7
  463.0 62.1 reduce-scatter.4
where the time goes:
time: 535 us
  waiting for transfers between devices  328 us (61%)
  other arithmetic  89.2 us (17%)
  blocking collectives  73.7 us (14%)
  matrix products  24.1 us (5%)
  between operations  15.9 us (3%)
    psum x1, waiting for transfers between devices, per_device(): gram_matrix = lax.psum(gram_part, 'pcol') / order_full  108 us
    reduce_scatter x1, waiting for transfers between devices, per_device(): lax.psum_scatter(-jnp.einsum('ijbr,ijrt->bit', left_factor, weights, pref...  66.3 us
    psum x1, blocking collectives, per_device(): target_correlation = lax.psum(correlation_part, 'pcol').astype(jnp.bfloat16)  49.8 us
    all_gather x1, waiting for transfers between devices, per_device(): lax.all_gather(pivot_right, 'prow', axis=1, tiled=True)  48.8 us
    another operation x4, other arithmetic, per_device(): lower_factor = jnp.linalg.cholesky(gram_matrix)  47.1 us
    all_gather x1, waiting for transfers between devices, per_device(): lax.all_gather(basis_rows.astype(jnp.bfloat16), 'pcol', axis=0, tiled=True)  40.2 us
    another operation x3, other arithmetic, solve_rows(): lax.linalg.triangular_solve(lower_factor, stacked, left_side=False, lower...  39.4 us
    psum x1, waiting for transfers between devices, per_device(): target_sample = lax.psum(sample_part, 'pcol')  27.8 us
  transfers between devices with their start and end apart: 7, of which 7 were waited for; matrix products, arithmetic and copies ran while one was open for 3% of the time, Pallas kernels for 0%

commit v1 on v0

--- a/solution.py
+++ b/solution.py
@@ -70,7 +70,9 @@
     correlation_part = jnp.einsum(
         "bis,bit->ist", target_left, basis_half, preferred_element_type=jnp.float32
     )
-    target_correlation = lax.psum(correlation_part, "pcol").astype(jnp.bfloat16)
+    target_correlation = jnp.sum(lax.all_gather(correlation_part, "pcol"), axis=0).astype(
+        jnp.bfloat16
+    )
     projected = lax.psum_scatter(
         -jnp.einsum("jbs,ijst->bit", pivot_whole, reduced, preferred_element_type=jnp.float32),
         "pcol",

time: 535 us -> 573 us (1.071)
  waiting for transfers between devices: 328 us -> 410 us
  blocking collectives: 73.7 us -> 24.1 us
    reduce_scatter x1, waiting for transfers between devices: 11.4 us -> 61.8 us  [per_device(): lax.psum_scatter(-jnp.einsum('jbs,ijst->bit', pivot_whole, reduced, prefe...]
    psum x1 -> x0, blocking collectives: 49.8 us -> none  [per_device(): target_correlation = lax.psum(correlation_part, 'pcol').astype(jnp.bfloat16)]
    all_gather x0 -> x1, waiting for transfers between devices: none -> 34.4 us  [per_device(): lax.all_gather(correlation_part, 'pcol')]
  transfers between devices with their start and end apart: 7 -> 8, of which waited for: 7 -> 8; matrix products, arithmetic and copies ran while one was open for 3% -> 5% of each run, Pallas kernels for 0% -> 0%
where the time goes in v1:
time: 573 us; the launch traced here: 572 us
  waiting for transfers between devices  410 us (72%)
  other arithmetic  91.6 us (16%)
  matrix products  25 us (4%)
  blocking collectives  24.1 us (4%)
  between operations  15.7 us (3%)
  local copies, waits for them, and re-layouts  5.87 us (1%)
    psum x1, waiting for transfers between devices, per_device(): gram_matrix = lax.psum(gram_part, 'pcol') / order_full  108 us
    reduce_scatter x1, waiting for transfers between devices, per_device(): lax.psum_scatter(-jnp.einsum('ijbr,ijrt->bit', left_factor, weights, pref...  66.3 us
    reduce_scatter x1, waiting for transfers between devices, per_device(): lax.psum_scatter(-jnp.einsum('jbs,ijst->bit', pivot_whole, reduced, prefe...  61.8 us
    all_gather x1, waiting for transfers between devices, per_device(): lax.all_gather(pivot_right, 'prow', axis=1, tiled=True)  48.3 us
    another operation x4, other arithmetic, per_device(): lower_factor = jnp.linalg.cholesky(gram_matrix)  47.1 us
    another operation x3, other arithmetic, solve_rows(): lax.linalg.triangular_solve(lower_factor, stacked, left_side=False, lower...  39.4 us
    all_gather x1, waiting for transfers between devices, per_device(): lax.all_gather(basis_rows.astype(jnp.bfloat16), 'pcol', axis=0, tiled=True)  38.1 us
    all_gather x1, waiting for transfers between devices, per_device(): lax.all_gather(correlation_part, 'pcol')  34.4 us
  transfers between devices with their start and end apart: 8, of which 8 were waited for; matrix products, arithmetic and copies ran while one was open for 5% of the time, Pallas kernels for 0%

profile of v1, /device:TPU:6, one launch (start us, length us, event | category | flops | bytes accessed | tf_op | source)
XLA Modules:
  0.0 572.5 jit_solution(2333357237123412623)
XLA Ops:
  8.1 1.6 copy.62
  9.7 1.6 copy.63
  11.4 24.1 %all_gather.19 = bf16[2048,128]{1,0:T(8,128)(2,1)S(1)} all-gather(bf16[128,128]{1,0:T(8,128)(2,1)} %param.14), channel_id=1, replica_groups=mesh['prow'=16,'pcol'=16] {'prow'}, dimensions={0}, use_global_device_ids=true | all-gather | bytes 557056 | tf_op jit(solution)/shard_map/all_gather | solution.py:23
  35.5 1.8 convolution_bitcast_fusion.4
  37.4 0.8 fusion.34
  38.2 24.5 %all-gather.6.cloned.1.call-done = bf16[2,2048,128]{1,2,0:T(8,128)(2,1)} async-done(((bf16[2,128,128]{1,2,0:T(8,128)(2,1)}), bf16[2,2048,128]{1,2,0:T(8,128)(2,1)}) %all-gather.6.cloned.1.call-update) | async-done | bytes 1048592 | tf_op jit(solution)/shard_map/all_gather | solution.py:21
  62.7 1.7 convolution_bitcast_fusion.5
  64.4 48.3 %all-gather.8.cloned.1.call-done = bf16[2,2048,128]{1,2,0:T(8,128)(2,1)} async-done(((bf16[2,128,128]{1,2,0:T(8,128)(2,1)}), bf16[2,2048,128]{1,2,0:T(8,128)(2,1)}) %all-gather.8.cloned.1.call-update) | async-done | bytes 1048592 | tf_op jit(solution)/shard_map/all_gather | solution.py:22
  112.7 3.4 fusion.12
  116.7 3.4 fusion.1
  120.2 28.2 %all-reduce.3.cloned.1.call-done = f32[4,128,128]{1,2,0:T(8,128)} async-done(((f32[4,128,128]{1,2,0:T(8,128)}), f32[4,128,128]{1,2,0:T(8,128)}) %all-reduce.3.cloned.1.call-update) | async-done | bytes 262160 | tf_op jit(solution)/shard_map/psum | solution.py:33
  148.4 66.3 %reduce-scatter.3.cloned.1.call-done = f32[128,4,128]{0,2,1:T(8,128)} async-done(((f32[2048,4,128]{0,2,1:T(8,128)}), f32[128,4,128]{0,2,1:T(8,128)}) %reduce-scatter.3.cloned.1.call-update) | async-done | bytes 262160 | tf_op jit(solution)/shard_map/reduce_scatter | solution.py:50
  214.7 1.4 fusion.16
  216.1 1.4 fusion.37
  217.6 107.9 %all-reduce.5.cloned.1.call-done = f32[4,128,128]{1,2,0:T(8,128)} async-done(((f32[4,128,128]{1,2,0:T(8,128)}), f32[4,128,128]{1,2,0:T(8,128)}) %all-reduce.5.cloned.1.call-update) | async-done | bytes 262160 | tf_op jit(solution)/shard_map/psum | solution.py:59
  325.5 1.0 broadcast_multiply_fusion
  326.6 1.0 fusion.25
  327.6 46.9 %custom-call.7 = f32[4,128,128]{2,1,0:T(8,128)S(1)} custom-call(f32[4,128,128]{2,1,0:T(8,128)S(1)} %fusion.25), custom_call_target="Cholesky" | custom-call | tf_op jit(solution)/shard_map/jit(cholesky)/cholesky | solution.py:60
  374.8 39.3 %custom-call.8 = f32[4,1,128,128]{2,3,1,0:T(8,128)S(1)} custom-call(f32[4,1,128,128]{3,2,1,0:T(8,128)S(1)} %select_bitcast_fusion), custom_call_target="InvertDiagBlocksLowerTriangular" | custom-call | tf_op jit(solution)/shard_map/triangular_solve | solution.py:11
  414.1 1.3 fusion.36
  415.4 1.1 convolution_bitcast_fusion.3
  416.6 0.8 copy.82
  417.7 38.1 %all-gather.10.cloned.1.call-done = bf16[2048,4,128]{2,0,1:T(8,128)(2,1)} async-done(((bf16[128,4,128]{2,0,1:T(8,128)(2,1)}), bf16[2048,4,128]{2,0,1:T(8,128)(2,1)}) %all-gather.10.cloned.1.call-update) | async-done | bytes 2097168 | tf_op jit(solution)/shard_map/all_gather | solution.py:62
  455.8 3.8 fusion.6
  459.5 1.2 convolution_convert_fusion.1
  460.8 2.7 fusion
  463.5 0.9 copy.85
  464.4 34.4 %all-gather.12.cloned.1.call-done = f32[64,128,128]{2,1,0:T(8,128)} async-done(((f32[4,128,128]{2,1,0:T(8,128)}), f32[64,128,128]{2,1,0:T(8,128)}) %all-gather.12.cloned.1.call-update) | async-done | bytes 4194320 | tf_op jit(solution)/shard_map/all_gather | solution.py:73
  498.8 2.4 reduce_sum.9
  501.2 61.8 %reduce-scatter.5.cloned.1.call-done = f32[128,4,128]{0,2,1:T(8,128)} async-done(((f32[2048,4,128]{0,2,1:T(8,128)}), f32[128,4,128]{0,2,1:T(8,128)}) %reduce-scatter.5.cloned.1.call-update) | async-done | bytes 262160 | tf_op jit(solution)/shard_map/reduce_scatter | solution.py:76
  563.0 1.2 fusion.18
  564.2 0.8 copy.86
  (31 shorter events, 1.7 us)
Async XLA Ops:
  8.0 206.7 %copy-start = (bf16[128,4,128]{2,1,0:T(4,128)(2,1)S(1)}, bf16[128,4,128]{2,1,0:T(4,128)(2,1)}, u32[]{:S(2)}) copy-start(bf16[128,4,128]{2,1,0:T(4,128)(2,1)} %param.12) | copy-start | bytes 393220
  8.0 54.7 %all-gather.6.cloned.1.call-start = ((), (), s32[]{:S(2)}) async-start(), calls=%async_computation.2 | async-start | bytes 1114112 | tf_op jit(solution)/shard_map/all_gather | solution.py:21
  9.7 103.0 %all-gather.8.cloned.1.call-start = ((), (), s32[]{:S(2)}) async-start(), calls=%async_computation.3 | async-start | bytes 1114112 | tf_op jit(solution)/shard_map/all_gather | solution.py:22
  11.3 137.1 %all-reduce.3.cloned.1.call-start = ((), (), s32[]{:S(2)}) async-start(), calls=%async_computation.5 | async-start | bytes 524288 | tf_op jit(solution)/shard_map/psum | solution.py:33
  37.4 177.3 %reduce-scatter.3.cloned.1.call-start = ((), (), s32[]{:S(2)}) async-start(), calls=%async_computation.4 | async-start | bytes 4456448 | tf_op jit(solution)/shard_map/reduce_scatter | solution.py:50
  112.7 4.0 copy-start.1
  120.1 205.4 %all-reduce.5.cloned.1.call-start = ((), (), s32[]{:S(2)}) async-start(), calls=%async_computation.6 | async-start | bytes 524288 | tf_op jit(solution)/shard_map/psum | solution.py:59
  217.5 238.3 %all-gather.10.cloned.1.call-start = ((), (), s32[]{:S(2)}) async-start(), calls=%async_computation.7 | async-start | bytes 2228224 | tf_op jit(solution)/shard_map/all_gather | solution.py:62
  415.4 83.4 %all-gather.12.cloned.1.call-start = ((), (), s32[]{:S(2)}) async-start(), calls=%async_computation.9 | async-start | bytes 4456448 | tf_op jit(solution)/shard_map/all_gather | solution.py:73
  417.4 43.4 %copy-start.2 = (bf16[2,2048,128]{1,2,0:T(8,128)(2,1)S(1)}, bf16[2,2048,128]{1,2,0:T(8,128)(2,1)}, u32[]{:S(2)}) copy-start(bf16[2,2048,128]{1,2,0:T(8,128)(2,1)} %all-gather.6.cloned.1.call-done) | copy-start | bytes 3145732
  417.4 145.6 %reduce-scatter.5.cloned.1.call-start = ((), (), s32[]{:S(2)}) async-start(), calls=%async_computation.8 | async-start | bytes 4456448 | tf_op jit(solution)/shard_map/reduce_scatter | solution.py:76
  463.5 99.5 %copy-start.3 = (bf16[128,4,128]{2,1,0:T(4,128)(2,1)S(1)}, bf16[128,4,128]{2,1,0:T(4,128)(2,1)}, u32[]{:S(2)}) copy-start(bf16[128,4,128]{2,1,0:T(4,128)(2,1)} %param.13) | copy-start | bytes 393220
Sparse Core Ops, SparseCore 0:
  11.8 50.8 all-gather.5
  65.1 47.5 all-gather.7
Sparse Core Ops, SparseCore 1:
  37.4 110.9 all-reduce.2
  150.8 63.8 reduce-scatter.2
  217.6 107.9 all-reduce.4
  415.5 40.3 all-gather.9
  458.2 40.5 all-gather.11
  501.3 61.6 reduce-scatter.4
